TPU v7x, 32 devices: a whole 2x2x4 slice. The times are simulated.
32 devices in a mesh: copies: 2 (over y), blk: 4 (over x, core), virt: 4 (over z).
Axes of the slice: x: 2, y: 2, z: 4, core: 2. Of those that a mesh axis runs over, the one named last changes fastest.
Arguments:
- three_index: bfloat16 [32, 512, 2048], P(('copies', 'blk'), 'virt'), parts along dimension 0, may hold values from -0.59765625 to 0.59765625
- occ_energy: float32 [32], P(('copies', 'blk')), parts along dimension 0, may hold values from -2 to -0.5
- virt_energy: float32 [1024], P('copies'), parts along dimension 0, may hold values from 0.3 to 3
Outputs:
- gradient: bfloat16 [32, 512, 2048], P(('copies', 'blk'), 'virt'), parts along dimension 0
There are 2 independent parts, one for each index of `copies`. A program takes and returns all parts, laid end to end along the dimension named above; each array names one. Nothing has to cross between parts.
All inputs are finite; a program needn't handle non-finite values.
Results may differ from a plain program's by a relative error of at most 0.0055.
Values may be sent and summed in bfloat16 or wider, within the bound.
A program may use at most 64 MiB of HBM per device.

v0:
```python
import jax
import jax.numpy as jnp
from jax import lax
from jax.sharding import PartitionSpec as P


def shifted(shard, axis, by):
    devices = lax.axis_size(axis)
    return lax.ppermute(shard, axis, [(i, (i + by) % devices) for i in range(devices)])


def contract(left, right):
    return lax.dot_general(
        left, right, (((1,), (1,)), ((), ())), preferred_element_type=jnp.float32
    )


def pair_block(
    own_rows,
    part_full,
    part_rows,
    own_full,
    energy_own,
    energy_part,
    energy_rows,
    virt_energy,
    diagonal,
):
    occ_count, rows_here, aux_count = own_rows.shape
    virt_count = part_full.shape[1]
    first = contract(
        own_rows.reshape(occ_count * rows_here, aux_count),
        part_full.reshape(occ_count * virt_count, aux_count),
    )
    first = first.reshape(occ_count, rows_here, occ_count, virt_count)
    if diagonal:
        second = first.transpose(2, 1, 0, 3)
    else:
        second = contract(
            part_rows.reshape(occ_count * rows_here, aux_count),
            own_full.reshape(occ_count * virt_count, aux_count),
        )
        second = second.reshape(occ_count, rows_here, occ_count, virt_count).transpose(2, 1, 0, 3)
    denom = (
        energy_own[:, None, None, None]
        + energy_part[None, None, :, None]
        - energy_rows[None, :, None, None]
        - virt_energy[None, None, None, :]
    )
    tbar = ((2.0 * first - second) / denom).astype(jnp.bfloat16)
    flat = tbar.reshape(occ_count * rows_here, occ_count * virt_count)
    own = jnp.dot(
        flat,
        part_full.reshape(occ_count * virt_count, aux_count),
        preferred_element_type=jnp.float32,
    )
    return (tbar, first, own.reshape(occ_count, rows_here, aux_count))


def local(three_index, occ_energy, virt_energy):
    occ_count, rows_here, aux_count = three_index.shape
    virt_count = virt_energy.shape[0]
    row_start = lax.axis_index("virt") * rows_here
    energy_rows = lax.dynamic_slice_in_dim(virt_energy, row_start, rows_here, 0)
    own_full = lax.all_gather(three_index, "virt", axis=1, tiled=True)
    part_full, energy_part = (
        shifted(own_full, "blk", 1),
        shifted(occ_energy.astype(jnp.bfloat16), "blk", 1).astype(occ_energy.dtype),
    )
    part_rows = lax.dynamic_slice_in_dim(part_full, row_start, rows_here, 1)
    unused_tbar, unused_first, diag_own = pair_block(
        three_index,
        own_full,
        three_index,
        own_full,
        occ_energy,
        occ_energy,
        energy_rows,
        virt_energy,
        True,
    )
    tbar, first, cross_own = pair_block(
        three_index,
        part_full,
        part_rows,
        own_full,
        occ_energy,
        energy_part,
        energy_rows,
        virt_energy,
        False,
    )
    tiles = lax.all_to_all(tbar, "virt", split_axis=3, concat_axis=1, tiled=True)
    partial_value = lax.dot_general(
        tiles.reshape(occ_count * virt_count, occ_count * rows_here),
        own_full.reshape(occ_count * virt_count, aux_count),
        (((0,), (0,)), ((), ())),
        preferred_element_type=jnp.float32,
    )
    summed = partial_value.reshape(occ_count, rows_here, aux_count).astype(jnp.bfloat16)
    partner = shifted(summed, "blk", -1)
    return (diag_own + cross_own + partner.astype(jnp.float32)).astype(jnp.bfloat16)


def solution(mesh):
    placed = (P(("copies", "blk"), "virt", None), P(("copies", "blk")), P("copies"))
    return jax.shard_map(
        local,
        mesh=mesh,
        in_specs=placed,
        out_specs=P(("copies", "blk"), "virt", None),
        check_vma=False,
    )
```

profile of v0, /device:TPU:1, one launch (start us, length us, event | category | flops | bytes accessed | tf_op | source)
XLA Modules:
  0.0 382.6 jit_solution(1829108738289670631)
XLA Ops:
  6.5 0.7 all-gather.2.cloned.1.call-update
  7.3 153.5 %all-gather.2.cloned.1.call-done = bf16[4,512,2048]{2,1,0:T(8,128)(2,1)} async-done(((bf16[4,128,2048]{2,1,0:T(8,128)(2,1)}), bf16[4,512,2048]{2,1,0:T(8,128)(2,1)}) %all-gather.2.cloned.1.call-update) | async-done | bytes 8388624 | tf_op jit(solution)/shard_map/all_gather | solution.py:65
  160.8 1.6 collective-permute-start
  162.4 0.7 convert_element_type.22
  163.0 0.0 collective-permute-start.1
  163.0 0.8 dynamic_slice.6
  163.8 89.3 %collective-permute-done.1 = bf16[4]{0:T(256)(128)(2,1)S(1)} collective-permute-done((bf16[4]{0:T(256)(128)(2,1)S(1)}, bf16[4]{0:T(256)(128)(2,1)S(1)}, u32[]{:S(2)}, u32[]{:S(2)}) %collective-permute-start.1) | collective-permute-done | bytes 40 | tf_op jit(solution)/shard_map/ppermute | solution.py:9
  253.1 0.8 broadcast_add_fusion
  253.9 0.1 broadcast_subtract_fusion
  254.0 0.0 collective-permute-done
  254.0 7.9 %fusion.2 = f32[4,128,4,512]{3,1,0,2:T(8,128)S(1)} fusion(bf16[4,512,2048]{2,1,0:T(8,128)(2,1)} %collective-permute-done, bf16[4,128,2048]{2,1,0:T(8,128)(2,1)} %param.3), kind=kOutput, calls=%fused_computation.2 | convolution fusion | flops 4294967296 | bytes 14680064 | tf_op jit(solution)/shard_map/dot_general | solution.py:13
  261.9 6.9 %fusion.13 = bf16[4,128,4,512]{3,1,0,2:T(8,128)(2,1)S(1)} fusion(f32[4,128,4,512]{3,1,0,2:T(8,128)S(1)} %fusion.2, bf16[4,512,2048]{2,1,0:T(8,128)(2,1)S(1)} %bitcast.76, f32[4,128,4]{1,0,2:T(4,128)S(1)} %get-tuple-element.5, bf16[4,512,2048]{2,1,0:T(8,128)(2,1)} %collective-permute-done, s32[]{:T(128)S(6)} %select_n.4, f32[512]{0:T(512)S(1)} %copy-done.3), kind=kOutput, calls=%fused_computation.15 | convolution fusion | flops 4300210176 | bytes 16787460 | tf_op jit(solution)/shard_map/dot_general | solution.py:13
  268.8 1.3 copy-done.1
  270.1 3.1 copy.16
  273.2 50.8 %all_to_all.15 = bf16[4,128,4,512]{1,0,2,3:T(4,128)(2,1)S(1)} all-to-all(bf16[4,128,4,512]{1,0,2,3:T(4,128)(2,1)} %copy.16), channel_id=1, replica_groups=mesh['copies'=2,'blk'=4,'virt'=4] {'virt'}, dimensions={3} | all-to-all | bytes 4194304 | tf_op jit(solution)/shard_map/all_to_all | solution.py:93
  324.0 3.1 copy.17
  327.1 2.0 copy.30
  329.0 2.4 copy.18
  331.4 8.7 %convolution_convert_fusion = bf16[4,128,2048]{2,1,0:T(8,128)(2,1)S(1)} fusion(bf16[4,128,2048]{2,1,0:T(8,128)(2,1)} %bitcast.73, bf16[2048,2048,1]{1,0,2:T(8,128)(2,1)} %bitcast.74), kind=kOutput, calls=%fused_computation.20 | convolution fusion | flops 4296015872 | bytes 12582912 | tf_op jit(solution)/shard_map/dot_general | solution.py:94
  340.0 2.2 collective-permute-start.2
  342.2 6.9 %fusion.8 = f32[4,128,4,512]{3,1,2,0:T(8,128)S(1)} fusion(bf16[4,512,2048]{2,1,0:T(8,128)(2,1)} %all-gather.2.cloned.1.call-done, bf16[4,128,2048]{2,1,0:T(8,128)(2,1)S(1)} %copy-done), kind=kOutput, calls=%fused_computation.8 | convolution fusion | flops 4294967296 | bytes 14680064 | tf_op jit(solution)/shard_map/dot_general | solution.py:13
  349.2 7.5 %fusion.4 = f32[4,128,2048,1]{2,1,0,3:T(8,128)S(1)} fusion(bf16[4,512,2048]{2,1,0:T(8,128)(2,1)} %all-gather.2.cloned.1.call-done, f32[4,128,4,512]{3,1,2,0:T(8,128)S(1)} %fusion.8, f32[512]{0:T(512)S(1)} %copy-done.3, f32[4,128,4]{1,0,2:T(4,128)S(1)} %get-tuple-element.6), kind=kOutput, calls=%fused_computation.4 | convolution fusion | flops 4300210176 | bytes 16787456 | tf_op jit(solution)/shard_map/dot_general | solution.py:52
  356.7 9.4 %collective-permute-done.2 = bf16[4,128,2048]{2,1,0:T(8,128)(2,1)S(1)} collective-permute-done((bf16[4,128,2048]{2,1,0:T(8,128)(2,1)S(1)}, bf16[4,128,2048]{2,1,0:T(8,128)(2,1)S(1)}, u32[]{:S(2)}, u32[]{:S(2)}) %collective-permute-start.2) | collective-permute-done | bytes 2097184 | tf_op jit(solution)/shard_map/ppermute | solution.py:9
  366.1 9.6 %fusion.11 = bf16[4,128,2048]{2,1,0:T(8,128)(2,1)} fusion(f32[4,128,2048,1]{2,1,0,3:T(8,128)S(1)} %fusion.4, bf16[4,128,2048]{2,1,0:T(8,128)(2,1)S(1)} %collective-permute-done.2, bf16[4,128,4,512]{3,1,0,2:T(8,128)(2,1)S(1)} %copy-done.2, bf16[4,512,2048]{2,1,0:T(8,128)(2,1)} %collective-permute-done), kind=kOutput, calls=%fused_computation.12 | convolution fusion | flops 4299161600 | bytes 18874368 | tf_op jit(solution)/shard_map/dot_general | solution.py:52
  (14 shorter events, 0.0 us)
Async XLA Ops:
  6.5 154.2 %all-gather.2.cloned.1.call-start = ((), (), s32[]{:S(2)}) async-start(), calls=%async_computation.1 | async-start | bytes 10485760 | tf_op jit(solution)/shard_map/all_gather | solution.py:65
  160.8 93.2 %collective-permute-start = (bf16[4,512,2048]{2,1,0:T(8,128)(2,1)}, bf16[4,512,2048]{2,1,0:T(8,128)(2,1)}, u32[]{:S(2)}, u32[]{:S(2)}) collective-permute-start(bf16[4,512,2048]{2,1,0:T(8,128)(2,1)} %all-gather.2.cloned.1.call-done), channel_id=1, source_target_pairs={{0,4},{4,8},{8,12},{12,0},{1,5},{5,9},{9,13},{13,1},{2,6},{6,10},{... | collective-permute-start | bytes 25165832 | tf_op jit(solution)/shard_map/ppermute | solution.py:9
  163.0 90.0 %collective-permute-start.1 = (bf16[4]{0:T(256)(128)(2,1)S(1)}, bf16[4]{0:T(256)(128)(2,1)S(1)}, u32[]{:S(2)}, u32[]{:S(2)}) collective-permute-start(bf16[4]{0:T(256)(128)(2,1)S(1)} %convert_element_type.22), channel_id=1, source_target_pairs={{0,4},{4,8},{8,12},{12,0},{1,5},{5,9},{9,13},{13,1},{2,6},{6,10},{... | collective-permute-start | bytes 32 | tf_op jit(solution)/shard_map/ppermute | solution.py:9
  253.9 8.0 %slice-start = ((s8[8388608]{0:T(1024)(128)(4,1)}), s8[4194304]{0:T(1024)(128)(4,1)S(1)}, s32[]{:S(2)}) async-start(s8[8388608]{0:T(1024)(128)(4,1)} %bitcast.75), calls=%async_computation.2 | async-start | bytes 8388608
  253.9 7.9 %slice-start.1 = ((s8[8388608]{0:T(1024)(128)(4,1)}), s8[4194304]{0:T(1024)(128)(4,1)S(1)}, s32[]{:S(2)}) async-start(s8[8388608]{0:T(1024)(128)(4,1)} %bitcast.75), calls=%async_computation.3 | async-start | bytes 8388608
  253.9 7.9 %copy-start.3 = (f32[512]{0:T(512)S(1)}, f32[512]{0:T(512)}, u32[]{:S(2)}) copy-start(f32[512]{0:T(512)} %param.5) | copy-start | bytes 6148
  268.8 1.3 copy-start.1
  331.4 10.8 %copy-start = (bf16[4,128,2048]{2,1,0:T(8,128)(2,1)S(1)}, bf16[4,128,2048]{2,1,0:T(8,128)(2,1)}, u32[]{:S(2)}) copy-start(bf16[4,128,2048]{2,1,0:T(8,128)(2,1)} %param.3) | copy-start | bytes 6291460
  340.0 26.1 %collective-permute-start.2 = (bf16[4,128,2048]{2,1,0:T(8,128)(2,1)S(1)}, bf16[4,128,2048]{2,1,0:T(8,128)(2,1)S(1)}, u32[]{:S(2)}, u32[]{:S(2)}) collective-permute-start(bf16[4,128,2048]{2,1,0:T(8,128)(2,1)S(1)} %convolution_convert_fusion), channel_id=1, source_target_pairs={{0,12},{4,0},{8,4},{12,8},{1,13},{5,1},{9,5},{13,9},{2,14},{6,2},{... | collective-permute-start | bytes 6291464 | tf_op jit(solution)/shard_map/ppermute | solution.py:9
  349.2 16.9 %copy-start.2 = (bf16[4,128,4,512]{3,1,0,2:T(8,128)(2,1)S(1)}, bf16[4,128,4,512]{3,1,0,2:T(8,128)(2,1)}, u32[]{:S(2)}) copy-start(bf16[4,128,4,512]{3,1,0,2:T(8,128)(2,1)} %copy-done.1) | copy-start | bytes 6291460
Sparse Core Ops, SparseCore 0:
  8.9 151.8 all-gather.1
where the time goes:
time: 383 us
  waiting for transfers between devices  253 us (66%)
  blocking collectives  50.8 us (13%)
  matrix products  47.5 us (12%)
  between operations  13.5 us (4%)
  local copies, waits for them, and re-layouts  12.6 us (3%)
    all_gather x1, waiting for transfers between devices, local(): own_full = lax.all_gather(three_index, 'virt', axis=1, tiled=True)  154 us
    ppermute x3, waiting for transfers between devices, shifted(): lax.ppermute(shard, axis, [(i, (i + by) % devices) for i in range(devices)])  98.7 us
    all_to_all x1, blocking collectives, local(): lax.all_to_all(tbar, 'virt', split_axis=3, concat_axis=1, tiled=True)  50.8 us
    dot_general x3, matrix products, contract(): lax.dot_general(left, right, (((1,), (1,)), ((), ())), preferred_element_...  21.7 us
    dot_general x2, matrix products, pair_block(): jnp.dot(flat, part_full.reshape(occ_count * virt_count, aux_count), prefe...  17.1 us
    dot_general x1, matrix products, local(): lax.dot_general(tiles.reshape(occ_count * virt_count, occ_count * rows_he...  8.65 us
  transfers between devices with their start and end apart: 4, of which 3 were waited for; matrix products, arithmetic and copies ran while one was open for 4% of the time, Pallas kernels for 0%

commit v1 on v0

--- a/solution.py
+++ b/solution.py
@@ -90,7 +90,9 @@
         virt_energy,
         False,
     )
-    tiles = lax.all_to_all(tbar, "virt", split_axis=3, concat_axis=1, tiled=True)
+    pieces = jnp.split(tbar, lax.axis_size("virt"), axis=3)
+    received = lax.all_to_all(jnp.stack(pieces), "virt", 0, 0)
+    tiles = jnp.concatenate(received, axis=1)
     partial_value = lax.dot_general(
         tiles.reshape(occ_count * virt_count, occ_count * rows_here),
         own_full.reshape(occ_count * virt_count, aux_count),

time: 383 us -> 379 us (0.990)
  local copies, waits for them, and re-layouts: 12.6 us -> 6.32 us
where the time goes in v1:
time: 379 us; the launch traced here: 378 us
  waiting for transfers between devices  253 us (67%)
  matrix products  50.5 us (13%)
  blocking collectives  49.7 us (13%)
  between operations  13.5 us (4%)
  local copies, waits for them, and re-layouts  6.32 us (2%)
    all_gather x1, waiting for transfers between devices, local(): own_full = lax.all_gather(three_index, 'virt', axis=1, tiled=True)  154 us
    ppermute x3, waiting for transfers between devices, shifted(): lax.ppermute(shard, axis, [(i, (i + by) % devices) for i in range(devices)])  98.7 us
    all_to_all x1, blocking collectives, local(): received = lax.all_to_all(jnp.stack(pieces), 'virt', 0, 0)  49.7 us
    dot_general x3, matrix products, contract(): lax.dot_general(left, right, (((1,), (1,)), ((), ())), preferred_element_...  24.8 us
    dot_general x2, matrix products, pair_block(): jnp.dot(flat, part_full.reshape(occ_count * virt_count, aux_count), prefe...  17 us
    dot_general x1, matrix products, local(): lax.dot_general(tiles.reshape(occ_count * virt_count, occ_count * rows_he...  8.65 us
  transfers between devices with their start and end apart: 4, of which 3 were waited for; matrix products, arithmetic and copies ran while one was open for 4% of the time, Pallas kernels for 0%

profile of v1, /device:TPU:1, one launch (start us, length us, event | category | flops | bytes accessed | tf_op | source)
XLA Modules:
  0.0 378.4 jit_solution(13730529247134128544)
XLA Ops:
  6.5 0.7 all-gather.2.cloned.1.call-update
  7.3 153.5 %all-gather.2.cloned.1.call-done = bf16[4,512,2048]{2,1,0:T(8,128)(2,1)} async-done(((bf16[4,128,2048]{2,1,0:T(8,128)(2,1)}), bf16[4,512,2048]{2,1,0:T(8,128)(2,1)}) %all-gather.2.cloned.1.call-update) | async-done | bytes 8388624 | tf_op jit(solution)/shard_map/all_gather | solution.py:65
  160.8 1.6 collective-permute-start
  162.4 0.7 convert_element_type.22
  163.0 0.0 collective-permute-start.1
  163.0 0.8 dynamic_slice.6
  163.8 89.3 %collective-permute-done.1 = bf16[4]{0:T(256)(128)(2,1)S(1)} collective-permute-done((bf16[4]{0:T(256)(128)(2,1)S(1)}, bf16[4]{0:T(256)(128)(2,1)S(1)}, u32[]{:S(2)}, u32[]{:S(2)}) %collective-permute-start.1) | collective-permute-done | bytes 40 | tf_op jit(solution)/shard_map/ppermute | solution.py:9
  253.1 0.8 broadcast_add_fusion
  253.9 0.1 broadcast_subtract_fusion
  254.0 10.7 %fusion.2 = f32[4,128,4,512]{3,1,0,2:T(8,128)} fusion(bf16[4,512,2048]{2,1,0:T(8,128)(2,1)} %collective-permute-done, bf16[4,128,2048]{2,1,0:T(8,128)(2,1)} %param.3), kind=kOutput, calls=%fused_computation.2 | convolution fusion | flops 4294967296 | bytes 14680064 | tf_op jit(solution)/shard_map/dot_general | solution.py:13
  264.6 7.2 %fusion.13 = bf16[4,128,4,512]{3,1,0,2:T(8,128)(2,1)S(1)} fusion(f32[4,128,4,512]{3,1,0,2:T(8,128)} %fusion.2, bf16[4,512,2048]{2,1,0:T(8,128)(2,1)S(1)} %bitcast.83, f32[4,128,4]{1,0,2:T(4,128)S(1)} %get-tuple-element.9, bf16[4,512,2048]{2,1,0:T(8,128)(2,1)} %collective-permute-done, s32[]{:T(128)S(6)} %select_n.4, f32[512]{0:T(512)S(1)} %copy-done.3), kind=kOutput, calls=%fused_computation.15 | convolution fusion | flops 4300210176 | bytes 16787460 | tf_op jit(solution)/shard_map/dot_general | solution.py:13
  271.9 0.6 slice_bitcast_fusion.3
  272.5 0.3 pad_maximum_fusion
  272.8 0.5 copy-done.1
  273.2 49.7 %all_to_all.5 = bf16[4,4,128,4,128]{4,2,1,3,0:T(8,128)(2,1)S(1)} all-to-all(bf16[4,4,128,4,128]{4,2,1,3,0:T(8,128)(2,1)S(1)} %pad_maximum_fusion), channel_id=1, replica_groups=mesh['copies'=2,'blk'=4,'virt'=4] {'virt'}, dimensions={0} | all-to-all | bytes 4194304 | tf_op jit(solution)/shard_map/all_to_all | solution.py:94
  322.9 1.8 copy.12
  324.7 0.4 copy.27
  325.0 2.4 copy.13
  327.4 8.7 %convolution_convert_fusion = bf16[4,128,2048]{2,1,0:T(8,128)(2,1)S(1)} fusion(bf16[4,128,2048]{2,1,0:T(8,128)(2,1)} %bitcast.80, bf16[2048,2048,1]{1,0,2:T(8,128)(2,1)} %bitcast.81), kind=kOutput, calls=%fused_computation.20 | convolution fusion | flops 4296015872 | bytes 12582912 | tf_op jit(solution)/shard_map/dot_general | solution.py:96
  336.1 2.0 collective-permute-start.2
  338.1 6.9 %fusion.8 = f32[4,128,4,512]{3,1,2,0:T(8,128)S(1)} fusion(bf16[4,512,2048]{2,1,0:T(8,128)(2,1)} %all-gather.2.cloned.1.call-done, bf16[4,128,2048]{2,1,0:T(8,128)(2,1)S(1)} %copy-done), kind=kOutput, calls=%fused_computation.8 | convolution fusion | flops 4294967296 | bytes 14680064 | tf_op jit(solution)/shard_map/dot_general | solution.py:13
  345.0 7.5 %fusion.4 = f32[4,128,2048,1]{2,1,0,3:T(8,128)S(1)} fusion(bf16[4,512,2048]{2,1,0:T(8,128)(2,1)} %all-gather.2.cloned.1.call-done, f32[4,128,4,512]{3,1,2,0:T(8,128)S(1)} %fusion.8, f32[512]{0:T(512)S(1)} %copy-done.3, f32[4,128,4]{1,0,2:T(4,128)S(1)} %get-tuple-element.10), kind=kOutput, calls=%fused_computation.4 | convolution fusion | flops 4300210176 | bytes 16787456 | tf_op jit(solution)/shard_map/dot_general | solution.py:52
  352.5 9.4 %collective-permute-done.2 = bf16[4,128,2048]{2,1,0:T(8,128)(2,1)S(1)} collective-permute-done((bf16[4,128,2048]{2,1,0:T(8,128)(2,1)S(1)}, bf16[4,128,2048]{2,1,0:T(8,128)(2,1)S(1)}, u32[]{:S(2)}, u32[]{:S(2)}) %collective-permute-start.2) | collective-permute-done | bytes 2097184 | tf_op jit(solution)/shard_map/ppermute | solution.py:9
  362.0 9.6 %fusion.11 = bf16[4,128,2048]{2,1,0:T(8,128)(2,1)} fusion(f32[4,128,2048,1]{2,1,0,3:T(8,128)S(1)} %fusion.4, bf16[4,128,2048]{2,1,0:T(8,128)(2,1)S(1)} %collective-permute-done.2, bf16[4,128,4,512]{3,1,0,2:T(8,128)(2,1)S(1)} %copy-done.2, bf16[4,512,2048]{2,1,0:T(8,128)(2,1)} %collective-permute-done), kind=kOutput, calls=%fused_computation.12 | convolution fusion | flops 4299161600 | bytes 18874368 | tf_op jit(solution)/shard_map/dot_general | solution.py:52
  (15 shorter events, 0.0 us)
Async XLA Ops:
  6.5 154.2 %all-gather.2.cloned.1.call-start = ((), (), s32[]{:S(2)}) async-start(), calls=%async_computation.1 | async-start | bytes 10485760 | tf_op jit(solution)/shard_map/all_gather | solution.py:65
  160.8 93.2 %collective-permute-start = (bf16[4,512,2048]{2,1,0:T(8,128)(2,1)}, bf16[4,512,2048]{2,1,0:T(8,128)(2,1)}, u32[]{:S(2)}, u32[]{:S(2)}) collective-permute-start(bf16[4,512,2048]{2,1,0:T(8,128)(2,1)} %all-gather.2.cloned.1.call-done), channel_id=1, source_target_pairs={{0,4},{4,8},{8,12},{12,0},{1,5},{5,9},{9,13},{13,1},{2,6},{6,10},{... | collective-permute-start | bytes 25165832 | tf_op jit(solution)/shard_map/ppermute | solution.py:9
  163.0 90.0 %collective-permute-start.1 = (bf16[4]{0:T(256)(128)(2,1)S(1)}, bf16[4]{0:T(256)(128)(2,1)S(1)}, u32[]{:S(2)}, u32[]{:S(2)}) collective-permute-start(bf16[4]{0:T(256)(128)(2,1)S(1)} %convert_element_type.22), channel_id=1, source_target_pairs={{0,4},{4,8},{8,12},{12,0},{1,5},{5,9},{9,13},{13,1},{2,6},{6,10},{... | collective-permute-start | bytes 32 | tf_op jit(solution)/shard_map/ppermute | solution.py:9
  253.9 10.8 %slice-start = ((s8[8388608]{0:T(1024)(128)(4,1)}), s8[4194304]{0:T(1024)(128)(4,1)S(1)}, s32[]{:S(2)}) async-start(s8[8388608]{0:T(1024)(128)(4,1)} %bitcast.82), calls=%async_computation.2 | async-start | bytes 8388608
  253.9 10.7 %slice-start.1 = ((s8[8388608]{0:T(1024)(128)(4,1)}), s8[4194304]{0:T(1024)(128)(4,1)S(1)}, s32[]{:S(2)}) async-start(s8[8388608]{0:T(1024)(128)(4,1)} %bitcast.82), calls=%async_computation.3 | async-start | bytes 8388608
  253.9 10.7 %copy-start.3 = (f32[512]{0:T(512)S(1)}, f32[512]{0:T(512)}, u32[]{:S(2)}) copy-start(f32[512]{0:T(512)} %param.5) | copy-start | bytes 6148
  271.9 1.3 copy-start.1
  327.4 10.7 %copy-start = (bf16[4,128,2048]{2,1,0:T(8,128)(2,1)S(1)}, bf16[4,128,2048]{2,1,0:T(8,128)(2,1)}, u32[]{:S(2)}) copy-start(bf16[4,128,2048]{2,1,0:T(8,128)(2,1)} %param.3) | copy-start | bytes 6291460
  336.1 25.9 %collective-permute-start.2 = (bf16[4,128,2048]{2,1,0:T(8,128)(2,1)S(1)}, bf16[4,128,2048]{2,1,0:T(8,128)(2,1)S(1)}, u32[]{:S(2)}, u32[]{:S(2)}) collective-permute-start(bf16[4,128,2048]{2,1,0:T(8,128)(2,1)S(1)} %convolution_convert_fusion), channel_id=1, source_target_pairs={{0,12},{4,0},{8,4},{12,8},{1,13},{5,1},{9,5},{13,9},{2,14},{6,2},{... | collective-permute-start | bytes 6291464 | tf_op jit(solution)/shard_map/ppermute | solution.py:9
  345.0 16.9 %copy-start.2 = (bf16[4,128,4,512]{3,1,0,2:T(8,128)(2,1)S(1)}, bf16[4,128,4,512]{3,1,0,2:T(8,128)(2,1)}, u32[]{:S(2)}) copy-start(bf16[4,128,4,512]{3,1,0,2:T(8,128)(2,1)} %copy-done.1) | copy-start | bytes 6291460
Sparse Core Ops, SparseCore 0:
  8.9 151.8 all-gather.1
